TPU v7x, 32 devices: a whole 2x2x4 slice. The times are simulated.
32 devices in a mesh: row: 8 (over y, x, core), col: 4 (over z).
Axes of the slice: x: 2, y: 2, z: 4, core: 2. Of those that a mesh axis runs over, the one named last changes fastest.
Arguments:
- dual_ops: float32 [8, 4, 2048, 2048], P('row', 'col'), as said below
- basis: float32 [8, 4, 4, 64, 512], P('row', 'col'), may hold values from -0.125 to 0.125
- coarse_inverse: float32 [2048, 2048], P('row', 'col')
- gap_rhs: float32 [8, 4, 4, 32, 512], P('row', 'col'), may hold values from -6 to 6
- coarse_rhs: float32 [8, 4, 32, 64], P('row', 'col'), may hold values from -6 to 6
- contact_mask: int32 [8, 4, 4, 512], P('row', 'col'), may hold values 0 or 1
Outputs:
- multipliers: float32 [8, 4, 4, 32, 512], P('row', 'col')
- projected_grad: float32 [8, 4, 4, 32, 512], P('row', 'col')
Inputs may be any that keep to these rules, and one draw needn't show every extreme that they name: `dual_ops`: each subdomain's dual operator is symmetric and positive definite.
All inputs are finite; a program needn't handle non-finite values. No bound on the sum of `contact_mask` on one device may be relied on, other than what follows from the above.
Results may differ from a plain program's by a relative error of at most 0.00025.
Values sent between devices are 32-bit elements; how exact they have to be, the bound alone decides.
A program may use at most 128 MiB of HBM per device.

v0:
```python
import jax
import jax.numpy as jnp
from jax import lax
from jax.sharding import PartitionSpec as P

MDEV = 64
ITERS = 6


HIGH = lax.Precision.HIGHEST


def padded(block, sides, width):
    for axis, dim in sides:
        count = lax.axis_size(axis)
        forward = [(i, i + 1) for i in range(count - 1)]
        backward = [(target, source) for source, target in forward]
        low = lax.ppermute(
            lax.slice_in_dim(block, block.shape[dim] - width, None, axis=dim), axis, forward
        )
        high = lax.ppermute(lax.slice_in_dim(block, 0, width, axis=dim), axis, backward)
        block = jnp.concatenate([low, block, high], axis=dim)
    return block


def neighbour_faces(values):
    rows_padded = padded(values[0:2], (("row", 0),), 1)
    cols_padded = padded(values[2:4], (("col", 0),), 1)
    return jnp.stack([rows_padded[0], rows_padded[3], cols_padded[0], cols_padded[3]], axis=0)


def shards(dual_ops, basis, coarse_inverse, gap_rhs, coarse_rhs, contact_mask):
    face_len = gap_rhs.shape[-1]
    blocks = dual_ops[0, 0].reshape(4, face_len, 4, face_len)
    local_basis = basis[0, 0]
    row_idx = lax.axis_index("row")
    col_idx = lax.axis_index("col")
    n_rows = lax.axis_size("row")
    n_cols = lax.axis_size("col")
    has_nb = jnp.stack([row_idx > 0, row_idx < n_rows - 1, col_idx > 0, col_idx < n_cols - 1])
    weight = jnp.where(has_nb, 0.5, 1.0).astype(jnp.float32)[:, None, None]
    contact = jnp.logical_and(contact_mask[0, 0] == 1, jnp.logical_not(has_nb)[:, None])[:, None, :]

    def apply_dual(vector):
        return jnp.einsum("gjfi,fki->gkj", blocks, vector, precision=HIGH)

    def coarse(coef):
        gathered = lax.all_gather(coef, "row", axis=1, tiled=True)
        partial_amps = lax.dot_general(
            gathered,
            coarse_inverse,
            (((1,), (1,)), ((), ())),
            precision=HIGH,
            preferred_element_type=jnp.float32,
        )
        summed = lax.psum(partial_amps, "col")
        return lax.dynamic_slice_in_dim(summed, col_idx * MDEV, MDEV, 1)

    def expand_sum(amps):
        own = jnp.einsum("fji,kj->fki", local_basis, amps, precision=HIGH)
        return own + neighbour_faces(own)

    local_rhs = gap_rhs[0, 0]
    dvec = local_rhs + neighbour_faces(local_rhs)
    multipliers = expand_sum(coarse(coarse_rhs[0, 0]))
    projected = jnp.zeros_like(multipliers)
    for step in range(ITERS):
        applied = apply_dual(multipliers)
        grad = applied + neighbour_faces(applied) - dvec
        projected = grad - expand_sum(
            coarse(jnp.einsum("fji,fki->kj", local_basis, grad, precision=HIGH))
        )
        image = apply_dual(projected)
        numer = jnp.sum(weight * grad * projected, axis=(0, 2))
        denom = jnp.sum(projected * image, axis=(0, 2))
        numer_all, denom_all = lax.psum((numer, denom), ("row", "col"))
        ratio = numer_all / denom_all
        multipliers = multipliers - ratio[None, :, None] * projected
        multipliers = jnp.where(contact, jnp.maximum(multipliers, 0.0), multipliers)
    return (multipliers[None, None], projected[None, None])


def solution(mesh):
    return jax.shard_map(
        shards,
        mesh=mesh,
        in_specs=(
            P("row", "col", None, None),
            P("row", "col", None, None, None),
            P("row", "col"),
            P("row", "col", None, None, None),
            P("row", "col", None, None),
            P("row", "col", None, None),
        ),
        out_specs=(P("row", "col", None, None, None), P("row", "col", None, None, None)),
        check_vma=False,
    )
```

profile of v0, /device:TPU:0, one launch (start us, length us, event | category | flops | bytes accessed | tf_op | source)
XLA Modules:
  0.0 938.7 jit_solution(12016818391664905516)
XLA Ops:
  13.9 19.3 %psum.133 = f32[32,256]{1,0:T(8,128)S(1)} all-reduce(f32[32,256]{1,0:T(8,128)S(1)} %fusion.178), channel_id=1, replica_groups=mesh['row'=8,'col'=4] {'col'}, use_global_device_ids=true, to_apply=%region_0.1 | all-reduce | flops 8192 | bytes 65536 | tf_op jit(solution)/shard_map/psum | solution.py:56
  47.3 20.4 %reshape_squeeze.3 = f32[4,512,4,512]{3,2,1,0:T(4,128)} reshape(f32[1,1,2048,2048]{3,2,1,0:T(8,128)} %param.6) | data formatting | bytes 33554432 | tf_op jit(solution)/shard_map/reshape;squeeze | solution.py:34
  75.3 24.6 %fusion.24 = f32[4,32,512]{2,1,0:T(8,128)S(1)} fusion(f32[4,512,4,512]{3,2,1,0:T(4,128)} %reshape_squeeze.3, f32[4,32,512]{2,1,0:T(8,128)S(1)} %convolution_bitcast_fusion.6, f32[1,32,512]{2,1,0:T(8,128)S(1)} %collective-permute-done.3, f32[1,32,512]{2,1,0:T(8,128)S(1)} %collective-permute-done.2, f32[1,32,512]{2,1,0:T(8,128)S(1)} %collective-permute-done.1, ...), kind=kOutput, calls=%fused_computation.24 | convolution fusion | flops 1610874880 | bytes 17563648 | tf_op jit(solution)/shard_map/gjfi,fki->gkj/dot_general | solution.py:45
  114.5 13.2 %all-gather.1 = f32[8,64,32]{1,2,0:T(8,128)S(1)} all-gather(f32[1,64,32]{1,2,0:T(8,128)S(1)} %convolution_bitcast_fusion.12), channel_id=1, replica_groups=mesh['row'=8,'col'=4] {'row'}, dimensions={0}, use_global_device_ids=true | all-gather | bytes 73728 | tf_op jit(solution)/shard_map/all_gather | solution.py:48
  128.5 16.0 %psum.134 = f32[32,256]{1,0:T(8,128)S(1)} all-reduce(f32[32,256]{1,0:T(8,128)S(1)} %fusion.179), channel_id=1, replica_groups=mesh['row'=8,'col'=4] {'col'}, use_global_device_ids=true, to_apply=%region_1.2 | all-reduce | flops 8192 | bytes 65536 | tf_op jit(solution)/shard_map/psum | solution.py:56
  156.7 22.3 %fusion.78 = f32[32]{0:T(128)S(1)} fusion(f32[4,32,512]{2,1,0:T(8,128)S(1)} %get-tuple-element.27, f32[4,512,4,512]{3,2,1,0:T(4,128)} %reshape_squeeze.3), kind=kOutput, calls=%fused_computation.49 | convolution fusion | flops 1610743808 | bytes 17039488 | tf_op jit(solution)/shard_map/gjfi,fki->gkj/dot_general | solution.py:45
  179.0 41.7 %all-reduce.5 = (f32[32]{0:T(128)S(1)}, f32[32]{0:T(128)S(1)}) all-reduce(f32[32]{0:T(128)S(1)} %get-tuple-element.26, f32[32]{0:T(128)S(1)} %fusion.78), channel_id=1, replica_groups=mesh['row'=8,'col'=4] {'row','col'}, use_global_device_ids=true, to_apply=%region_3.4 | all-reduce | flops 64 | bytes 512 | tf_op jit(solution)/shard_map/psum | solution.py:76
  220.8 24.6 %fusion.30 = f32[4,32,512]{2,1,0:T(8,128)S(1)} fusion(f32[4,512,4,512]{3,2,1,0:T(4,128)} %reshape_squeeze.3, f32[4,32,512]{2,1,0:T(8,128)S(1)} %maximum_select_fusion.5), kind=kOutput, calls=%fused_computation.26 | convolution fusion | flops 1610612736 | bytes 17301504 | tf_op jit(solution)/shard_map/gjfi,fki->gkj/dot_general | solution.py:45
  258.3 11.4 %all-gather.2 = f32[8,64,32]{1,2,0:T(8,128)S(1)} all-gather(f32[1,64,32]{1,2,0:T(8,128)S(1)} %convolution_bitcast_fusion.11), channel_id=1, replica_groups=mesh['row'=8,'col'=4] {'row'}, dimensions={0}, use_global_device_ids=true | all-gather | bytes 73728 | tf_op jit(solution)/shard_map/all_gather | solution.py:48
  270.4 17.6 %psum.137 = f32[32,256]{1,0:T(8,128)S(1)} all-reduce(f32[32,256]{1,0:T(8,128)S(1)} %fusion.180), channel_id=1, replica_groups=mesh['row'=8,'col'=4] {'col'}, use_global_device_ids=true, to_apply=%region_6.7 | all-reduce | flops 8192 | bytes 65536 | tf_op jit(solution)/shard_map/psum | solution.py:56
  300.3 22.3 %fusion.81 = f32[32]{0:T(128)S(1)} fusion(f32[4,32,512]{2,1,0:T(8,128)S(1)} %get-tuple-element.23, f32[4,512,4,512]{3,2,1,0:T(4,128)} %reshape_squeeze.3), kind=kOutput, calls=%fused_computation.50 | convolution fusion | flops 1610743808 | bytes 17039488 | tf_op jit(solution)/shard_map/gjfi,fki->gkj/dot_general | solution.py:45
  322.6 41.5 %all-reduce.4 = (f32[32]{0:T(128)S(1)}, f32[32]{0:T(128)S(1)}) all-reduce(f32[32]{0:T(128)S(1)} %get-tuple-element.22, f32[32]{0:T(128)S(1)} %fusion.81), channel_id=1, replica_groups=mesh['row'=8,'col'=4] {'row','col'}, use_global_device_ids=true, to_apply=%region_8.9 | all-reduce | flops 64 | bytes 512 | tf_op jit(solution)/shard_map/psum | solution.py:76
  364.1 24.4 %fusion.36 = f32[4,32,512]{2,1,0:T(8,128)S(1)} fusion(f32[4,512,4,512]{3,2,1,0:T(4,128)} %reshape_squeeze.3, f32[4,32,512]{2,1,0:T(8,128)S(1)} %maximum_select_fusion.5, f32[4,32,512]{2,1,0:T(8,128)S(1)} %get-tuple-element.23, f32[32]{0:T(128)S(1)} %div.19, pred[4,512]{1,0:T(4,128)(4,1)S(1)} %bitcast_and_fusion), kind=kOutput, calls=%fused_computation.28 | convolution fusion | flops 1610874880 | bytes 17565824 | tf_op jit(solution)/shard_map/gjfi,fki->gkj/dot_general | solution.py:45
  401.4 11.4 %all-gather.3 = f32[8,64,32]{1,2,0:T(8,128)S(1)} all-gather(f32[1,64,32]{1,2,0:T(8,128)S(1)} %convolution_bitcast_fusion.10), channel_id=1, replica_groups=mesh['row'=8,'col'=4] {'row'}, dimensions={0}, use_global_device_ids=true | all-gather | bytes 73728 | tf_op jit(solution)/shard_map/all_gather | solution.py:48
  413.5 17.9 %psum.140 = f32[32,256]{1,0:T(8,128)S(1)} all-reduce(f32[32,256]{1,0:T(8,128)S(1)} %fusion.181), channel_id=1, replica_groups=mesh['row'=8,'col'=4] {'col'}, use_global_device_ids=true, to_apply=%region_11.12 | all-reduce | flops 8192 | bytes 65536 | tf_op jit(solution)/shard_map/psum | solution.py:56
  443.7 22.3 %fusion.84 = f32[32]{0:T(128)S(1)} fusion(f32[4,32,512]{2,1,0:T(8,128)S(1)} %get-tuple-element.21, f32[4,512,4,512]{3,2,1,0:T(4,128)} %reshape_squeeze.3), kind=kOutput, calls=%fused_computation.51 | convolution fusion | flops 1610743808 | bytes 17039488 | tf_op jit(solution)/shard_map/gjfi,fki->gkj/dot_general | solution.py:45
  465.9 41.4 %all-reduce.3 = (f32[32]{0:T(128)S(1)}, f32[32]{0:T(128)S(1)}) all-reduce(f32[32]{0:T(128)S(1)} %get-tuple-element.20, f32[32]{0:T(128)S(1)} %fusion.84), channel_id=1, replica_groups=mesh['row'=8,'col'=4] {'row','col'}, use_global_device_ids=true, to_apply=%region_13.14 | all-reduce | flops 64 | bytes 512 | tf_op jit(solution)/shard_map/psum | solution.py:76
  507.5 24.6 %fusion.42 = f32[4,32,512]{2,1,0:T(8,128)S(1)} fusion(f32[4,512,4,512]{3,2,1,0:T(4,128)} %reshape_squeeze.3, f32[4,32,512]{2,1,0:T(8,128)S(1)} %maximum_select_fusion.3), kind=kOutput, calls=%fused_computation.30 | convolution fusion | flops 1610612736 | bytes 17301504 | tf_op jit(solution)/shard_map/gjfi,fki->gkj/dot_general | solution.py:45
  545.0 11.4 %all-gather.4 = f32[8,64,32]{1,2,0:T(8,128)S(1)} all-gather(f32[1,64,32]{1,2,0:T(8,128)S(1)} %convolution_bitcast_fusion.9), channel_id=1, replica_groups=mesh['row'=8,'col'=4] {'row'}, dimensions={0}, use_global_device_ids=true | all-gather | bytes 73728 | tf_op jit(solution)/shard_map/all_gather | solution.py:48
  557.2 17.7 %psum.143 = f32[32,256]{1,0:T(8,128)S(1)} all-reduce(f32[32,256]{1,0:T(8,128)S(1)} %fusion.182), channel_id=1, replica_groups=mesh['row'=8,'col'=4] {'col'}, use_global_device_ids=true, to_apply=%region_16.17 | all-reduce | flops 8192 | bytes 65536 | tf_op jit(solution)/shard_map/psum | solution.py:56
  587.1 22.3 %fusion.87 = f32[32]{0:T(128)S(1)} fusion(f32[4,32,512]{2,1,0:T(8,128)S(1)} %get-tuple-element.19, f32[4,512,4,512]{3,2,1,0:T(4,128)} %reshape_squeeze.3), kind=kOutput, calls=%fused_computation.52 | convolution fusion | flops 1610743808 | bytes 17039488 | tf_op jit(solution)/shard_map/gjfi,fki->gkj/dot_general | solution.py:45
  609.4 41.7 %all-reduce.2 = (f32[32]{0:T(128)S(1)}, f32[32]{0:T(128)S(1)}) all-reduce(f32[32]{0:T(128)S(1)} %get-tuple-element.18, f32[32]{0:T(128)S(1)} %fusion.87), channel_id=1, replica_groups=mesh['row'=8,'col'=4] {'row','col'}, use_global_device_ids=true, to_apply=%region_18.19 | all-reduce | flops 64 | bytes 512 | tf_op jit(solution)/shard_map/psum | solution.py:76
  651.1 24.4 %fusion.48 = f32[4,32,512]{2,1,0:T(8,128)S(1)} fusion(f32[4,512,4,512]{3,2,1,0:T(4,128)} %reshape_squeeze.3, f32[4,32,512]{2,1,0:T(8,128)S(1)} %maximum_select_fusion.3, f32[4,32,512]{2,1,0:T(8,128)S(1)} %get-tuple-element.19, f32[32]{0:T(128)S(1)} %div.21, pred[4,512]{1,0:T(4,128)(4,1)S(1)} %bitcast_and_fusion), kind=kOutput, calls=%fused_computation.32 | convolution fusion | flops 1610874880 | bytes 17565824 | tf_op jit(solution)/shard_map/gjfi,fki->gkj/dot_general | solution.py:45
  688.4 11.4 %all-gather.5 = f32[8,64,32]{1,2,0:T(8,128)S(1)} all-gather(f32[1,64,32]{1,2,0:T(8,128)S(1)} %convolution_bitcast_fusion.8), channel_id=1, replica_groups=mesh['row'=8,'col'=4] {'row'}, dimensions={0}, use_global_device_ids=true | all-gather | bytes 73728 | tf_op jit(solution)/shard_map/all_gather | solution.py:48
  700.5 17.6 %psum.146 = f32[32,256]{1,0:T(8,128)S(1)} all-reduce(f32[32,256]{1,0:T(8,128)S(1)} %fusion.183), channel_id=1, replica_groups=mesh['row'=8,'col'=4] {'col'}, use_global_device_ids=true, to_apply=%region_21.22 | all-reduce | flops 8192 | bytes 65536 | tf_op jit(solution)/shard_map/psum | solution.py:56
  730.4 22.3 %fusion.90 = f32[32]{0:T(128)S(1)} fusion(f32[4,32,512]{2,1,0:T(8,128)S(1)} %get-tuple-element.17, f32[4,512,4,512]{3,2,1,0:T(4,128)} %reshape_squeeze.3), kind=kOutput, calls=%fused_computation.53 | convolution fusion | flops 1610743808 | bytes 17039488 | tf_op jit(solution)/shard_map/gjfi,fki->gkj/dot_general | solution.py:45
  752.7 41.5 %all-reduce.1 = (f32[32]{0:T(128)S(1)}, f32[32]{0:T(128)S(1)}) all-reduce(f32[32]{0:T(128)S(1)} %get-tuple-element.16, f32[32]{0:T(128)S(1)} %fusion.90), channel_id=1, replica_groups=mesh['row'=8,'col'=4] {'row','col'}, use_global_device_ids=true, to_apply=%region_23.24 | all-reduce | flops 64 | bytes 512 | tf_op jit(solution)/shard_map/psum | solution.py:76
  794.4 24.6 %fusion.54 = f32[4,32,512]{2,1,0:T(8,128)S(1)} fusion(f32[4,512,4,512]{3,2,1,0:T(4,128)} %reshape_squeeze.3, f32[4,32,512]{2,1,0:T(8,128)S(1)} %maximum_select_fusion.1), kind=kOutput, calls=%fused_computation.34 | convolution fusion | flops 1610612736 | bytes 17301504 | tf_op jit(solution)/shard_map/gjfi,fki->gkj/dot_general | solution.py:45
  831.9 11.4 %all-gather.6 = f32[8,64,32]{1,2,0:T(8,128)S(1)} all-gather(f32[1,64,32]{1,2,0:T(8,128)S(1)} %convolution_bitcast_fusion.7), channel_id=1, replica_groups=mesh['row'=8,'col'=4] {'row'}, dimensions={0}, use_global_device_ids=true | all-gather | bytes 73728 | tf_op jit(solution)/shard_map/all_gather | solution.py:48
  844.0 17.7 %psum.149 = f32[32,256]{1,0:T(8,128)S(1)} all-reduce(f32[32,256]{1,0:T(8,128)S(1)} %fusion.184), channel_id=1, replica_groups=mesh['row'=8,'col'=4] {'col'}, use_global_device_ids=true, to_apply=%region_26.27 | all-reduce | flops 8192 | bytes 65536 | tf_op jit(solution)/shard_map/psum | solution.py:56
  874.0 22.4 %fusion.93 = f32[32]{0:T(128)S(1)} fusion(f32[4,32,512]{2,1,0:T(8,128)S(1)} %get-tuple-element.15, f32[4,512,4,512]{3,2,1,0:T(4,128)} %reshape_squeeze.3), kind=kOutput, calls=%fused_computation.54 | convolution fusion | flops 1610743808 | bytes 17039488 | tf_op jit(solution)/shard_map/gjfi,fki->gkj/dot_general | solution.py:45
  896.4 41.3 %all-reduce = (f32[32]{0:T(128)S(1)}, f32[32]{0:T(128)S(1)}) all-reduce(f32[32]{0:T(128)S(1)} %get-tuple-element.14, f32[32]{0:T(128)S(1)} %fusion.93), channel_id=1, replica_groups=mesh['row'=8,'col'=4] {'row','col'}, use_global_device_ids=true, to_apply=%region_28.29 | all-reduce | flops 64 | bytes 512 | tf_op jit(solution)/shard_map/psum | solution.py:76
  (195 shorter events, 192.5 us)
Async XLA Ops:
  33.6 34.2 %collective-permute-start = (f32[1,32,512]{2,1,0:T(8,128)S(1)}, f32[1,32,512]{2,1,0:T(8,128)S(1)}, u32[]{:S(2)}, u32[]{:S(2)}) collective-permute-start(f32[1,32,512]{2,1,0:T(8,128)S(1)} %get-tuple-element.82), channel_id=1, source_target_pairs={{0,4},{4,8},{8,12},{12,16},{16,20},{20,24},{24,28},{1,5},{5,9},{9,... | collective-permute-start | bytes 196616 | tf_op jit(solution)/shard_map/ppermute | solution.py:18
  34.9 34.3 %collective-permute-start.3 = (f32[1,32,512]{2,1,0:T(8,128)S(1)}, f32[1,32,512]{2,1,0:T(8,128)S(1)}, u32[]{:S(2)}, u32[]{:S(2)}) collective-permute-start(f32[1,32,512]{2,1,0:T(8,128)S(1)} %get-tuple-element.83), channel_id=1, source_target_pairs={{1,0},{2,1},{3,2},{5,4},{6,5},{7,6},{9,8},{10,9},{11,10},{13,12},{... | collective-permute-start | bytes 196616 | tf_op jit(solution)/shard_map/ppermute | solution.py:21
  36.2 34.3 %collective-permute-start.2 = (f32[1,32,512]{2,1,0:T(8,128)S(1)}, f32[1,32,512]{2,1,0:T(8,128)S(1)}, u32[]{:S(2)}, u32[]{:S(2)}) collective-permute-start(f32[1,32,512]{2,1,0:T(8,128)S(1)} %get-tuple-element.84), channel_id=1, source_target_pairs={{0,1},{1,2},{2,3},{4,5},{5,6},{6,7},{8,9},{9,10},{10,11},{12,13},{... | collective-permute-start | bytes 196616 | tf_op jit(solution)/shard_map/ppermute | solution.py:18
  40.8 34.5 %collective-permute-start.1 = (f32[1,32,512]{2,1,0:T(8,128)S(1)}, f32[1,32,512]{2,1,0:T(8,128)S(1)}, u32[]{:S(2)}, u32[]{:S(2)}) collective-permute-start(f32[1,32,512]{2,1,0:T(8,128)S(1)} %get-tuple-element.85), channel_id=1, source_target_pairs={{4,0},{8,4},{12,8},{16,12},{20,16},{24,20},{28,24},{5,1},{9,5},{13... | collective-permute-start | bytes 196616 | tf_op jit(solution)/shard_map/ppermute | solution.py:21
  43.0 60.6 %collective-permute-start.8 = (f32[1,32,512]{2,1,0:T(8,128)S(1)}, f32[1,32,512]{2,1,0:T(8,128)S(1)}, u32[]{:S(2)}, u32[]{:S(2)}) collective-permute-start(f32[1,32,512]{2,1,0:T(8,128)S(1)} %get-tuple-element.74), channel_id=1, source_target_pairs={{0,4},{4,8},{8,12},{12,16},{16,20},{20,24},{24,28},{1,5},{5,9},{9,... | collective-permute-start | bytes 196616 | tf_op jit(solution)/shard_map/ppermute | solution.py:18
  67.8 37.1 %collective-permute-start.9 = (f32[1,32,512]{2,1,0:T(8,128)S(1)}, f32[1,32,512]{2,1,0:T(8,128)S(1)}, u32[]{:S(2)}, u32[]{:S(2)}) collective-permute-start(f32[1,32,512]{2,1,0:T(8,128)S(1)} %get-tuple-element.75), channel_id=1, source_target_pairs={{4,0},{8,4},{12,8},{16,12},{20,16},{24,20},{28,24},{5,1},{9,5},{13... | collective-permute-start | bytes 196616 | tf_op jit(solution)/shard_map/ppermute | solution.py:21
  69.2 40.3 %collective-permute-start.11 = (f32[1,32,512]{2,1,0:T(8,128)S(1)}, f32[1,32,512]{2,1,0:T(8,128)S(1)}, u32[]{:S(2)}, u32[]{:S(2)}) collective-permute-start(f32[1,32,512]{2,1,0:T(8,128)S(1)} %get-tuple-element.76), channel_id=1, source_target_pairs={{1,0},{2,1},{3,2},{5,4},{6,5},{7,6},{9,8},{10,9},{11,10},{13,12},{... | collective-permute-start | bytes 196616 | tf_op jit(solution)/shard_map/ppermute | solution.py:21
  70.5 40.4 %collective-permute-start.10 = (f32[1,32,512]{2,1,0:T(8,128)S(1)}, f32[1,32,512]{2,1,0:T(8,128)S(1)}, u32[]{:S(2)}, u32[]{:S(2)}) collective-permute-start(f32[1,32,512]{2,1,0:T(8,128)S(1)} %get-tuple-element.77), channel_id=1, source_target_pairs={{0,1},{1,2},{2,3},{4,5},{5,6},{6,7},{8,9},{9,10},{10,11},{12,13},{... | collective-permute-start | bytes 196616 | tf_op jit(solution)/shard_map/ppermute | solution.py:18
  99.9 11.0 %collective-permute-start.4 = (f32[1,32,512]{2,1,0:T(8,128)S(1)}, f32[1,32,512]{2,1,0:T(8,128)S(1)}, u32[]{:S(2)}, u32[]{:S(2)}) collective-permute-start(f32[1,32,512]{2,1,0:T(8,128)S(1)} %get-tuple-element.78), channel_id=1, source_target_pairs={{0,4},{4,8},{8,12},{12,16},{16,20},{20,24},{24,28},{1,5},{5,9},{9,... | collective-permute-start | bytes 196616 | tf_op jit(solution)/shard_map/ppermute | solution.py:18
  103.6 7.3 collective-permute-start.7
  144.9 8.7 collective-permute-start.12
  146.2 7.4 collective-permute-start.15
  245.4 8.5 collective-permute-start.16
  246.7 7.2 collective-permute-start.19
  288.5 8.5 collective-permute-start.20
  289.8 7.2 collective-permute-start.23
  388.5 8.5 collective-permute-start.24
  389.8 7.2 collective-permute-start.27
  431.9 8.5 collective-permute-start.28
  433.2 7.2 collective-permute-start.31
  532.1 8.5 collective-permute-start.32
  533.4 7.2 collective-permute-start.35
  575.3 8.5 collective-permute-start.36
  576.6 7.2 collective-permute-start.39
  675.5 8.5 collective-permute-start.40
  676.8 7.2 collective-permute-start.43
  718.7 8.5 collective-permute-start.44
  720.0 7.2 collective-permute-start.47
  818.9 8.5 collective-permute-start.48
  820.2 7.2 collective-permute-start.51
  862.2 8.5 collective-permute-start.52
  863.5 7.2 collective-permute-start.55
  (29 other events, 380.3 us)
where the time goes:
time: 944 us; the launch traced here: 939 us
  blocking collectives  454 us (48%)
  matrix products  292 us (31%)
  starting transfers between devices  124 us (13%)
  waiting for transfers between devices  40.5 us (4%)
  local copies, waits for them, and re-layouts  23.6 us (2%)
    dot_general x12, matrix products, apply_dual(): return jnp.einsum('gjfi,fki->gkj', blocks, vector, precision=HIGH)  281 us
    psum x6, blocking collectives, shards(): numer_all, denom_all = lax.psum((numer, denom), ('row', 'col'))  249 us
    psum x7, blocking collectives, coarse(): summed = lax.psum(partial_amps, 'col')  124 us
    ppermute x28, starting transfers between devices, padded(): lax.ppermute(lax.slice_in_dim(block, block.shape[dim] - width, None, axis...  87.3 us
    all_gather x7, blocking collectives, coarse(): gathered = lax.all_gather(coef, 'row', axis=1, tiled=True)  80.8 us
    ppermute x28, starting transfers between devices, padded(): lax.ppermute(lax.slice_in_dim(block, 0, width, axis=dim), axis, backward)  36.5 us
    ppermute x28, waiting for transfers between devices, padded(): lax.ppermute(lax.slice_in_dim(block, 0, width, axis=dim), axis, backward)  34 us
    another operation x1, local copies, waits for them, and re-layouts, shards(): blocks = dual_ops[0, 0].reshape(4, face_len, 4, face_len)  20.4 us
  transfers between devices with their start and end apart: 56, of which 24 were waited for; matrix products, arithmetic and copies ran while one was open for 5% of the time, Pallas kernels for 0%

commit v1 on v0

v1 whole, which is shorter than its diff:
```python
import functools
import math

import jax
import jax.numpy as jnp
from jax import lax
from jax.experimental import pallas as pl
from jax.experimental.pallas import tpu as pltpu
from jax.sharding import PartitionSpec as P

ITERS = 6
MESH = pl.DeviceIdType.MESH
F32 = jnp.float32
BF16 = jnp.bfloat16


def split(x):
    hi = x.astype(BF16)
    return hi, (x - hi.astype(F32)).astype(BF16)


def dot(a, b, dims):
    return lax.dot_general(a, b, (dims, ((), ())), preferred_element_type=F32)


def dot3(x, hi, lo, dims):
    rows = x.shape[0]
    x_hi, x_lo = split(x)
    both = dot(jnp.concatenate([x_hi, x_lo], axis=0), hi, dims)
    return both[:rows] + (both[rows:] + dot(x_hi, lo, dims))


def pack(x):
    half = x.shape[0] // 2
    return jnp.concatenate([x[:half], x[half:]], axis=1)


def unpack(parts):
    n = parts[0].shape[1] // 2
    top = jnp.concatenate([p[:, :n] for p in parts], axis=1)
    return jnp.concatenate([top, jnp.concatenate([p[:, n:] for p in parts], axis=1)], axis=0)


def kernel(n_rows, n_cols, a_hbm, basis, cinv, gap, crhs, mask, m_out, p_out,
           stage, ahi, alo, bhi, blo, chi, clo, nbb, nbgap, halo_in, am, dvec, grad, image, xs, whi, wlo,
           ebuf, pout, pin, amp_s, nbamps, red_a, red_b,
           a_sem, bs, br, gs, gr, hs, hr, es, er, ps, pr, ams, amr, ras, rar, rbs, rbr):
    row = lax.axis_index("row")
    col = lax.axis_index("col")
    me = row * n_cols + col
    n_dev = n_rows * n_cols
    m_len = ahi.shape[0]
    _, k, face = halo_in.shape
    mdev = nbb.shape[1]
    width = red_a.shape[2]
    step_rows = m_len // a_sem.shape[0]
    n_blocks = a_sem.shape[0]
    has_nb = [row > 0, row < n_rows - 1, col > 0, col < n_cols - 1]
    nbr = [(row - 1, col), (row + 1, col), (row, col - 1), (row, col + 1)]

    def a_copy(i):
        rows = pl.ds(pl.multiple_of(i * step_rows, step_rows), step_rows)
        return pltpu.make_async_copy(a_hbm.at[0, 0, rows], stage.at[rows], a_sem.at[i])

    def a_start(i, carry):
        a_copy(i).start()
        return carry

    lax.fori_loop(0, n_blocks, a_start, 0)

    barrier = pltpu.get_barrier_semaphore()
    for d in range(1, n_dev):
        t = lax.rem(me + d, n_dev)
        pl.semaphore_signal(barrier, inc=1, device_id=(t // n_cols, lax.rem(t, n_cols)), device_id_type=MESH)
    pl.semaphore_wait(barrier, n_dev - 1)

    def remote(src, dst, ssem, rsem, where):
        return pltpu.make_async_remote_copy(
            src_ref=src, dst_ref=dst, send_sem=ssem, recv_sem=rsem, device_id=where, device_id_type=MESH)

    def face_start(f, src, dst, ssem, rsem):
        @pl.when(has_nb[f])
        def _():
            remote(src, dst.at[f ^ 1], ssem.at[f], rsem.at[f ^ 1], nbr[f]).start()

    def face_wait(f, src, dst, ssem, rsem):
        @pl.when(has_nb[f])
        def _():
            remote(src, dst.at[f], ssem.at[f], rsem.at[f], nbr[f]).wait()

    def basis_face(f):
        return basis.at[0, 0, f]

    def coarse(use, e, first=None, second=None, third=None):
        ebuf[use, row] = pack(e)
        copies = []
        for d in range(1, n_rows):
            copies.append(remote(ebuf.at[use, row], ebuf.at[use, row], es.at[use, d], er.at[use, d], (lax.rem(row + d, n_rows), col)))
            copies[-1].start()
        if first is not None:
            first()
        for copy in copies:
            copy.wait()
        gathered = unpack([ebuf[use, r] for r in range(n_rows)])
        partial = dot3(gathered, chi[...], clo[...], ((1,), (1,)))
        for c in range(n_cols):
            pout[c] = pack(partial[:, c * mdev:(c + 1) * mdev])
        copies = []
        for d in range(1, n_cols):
            c = lax.rem(col + d, n_cols)
            copies.append(remote(pout.at[c], pin.at[use, col], ps.at[use, d], pr.at[use, d], (row, c)))
            copies[-1].start()
        pin[use, col] = pout[col]
        if second is not None:
            second()
        for copy in copies:
            copy.wait()
        amps = pin[use, 0]
        for c in range(1, n_cols):
            amps = amps + pin[use, c]
        amp_s[...] = amps
        for f in range(4):
            face_start(f, amp_s, nbamps, ams, amr)
        if third is not None:
            third()
        for f in range(4):
            face_wait(f, amp_s, nbamps, ams, amr)
        return amps

    def expand_sum(amps, f):
        both = unpack([amps, nbamps[f]])
        return dot3(both, bhi[f], blo[f], ((1,), (0,)))

    def put_split(x, f):
        hi, lo = split(x)
        xs[0:k, f * face:(f + 1) * face] = hi
        xs[k:2 * k, f * face:(f + 1) * face] = lo

    def apply_face(f):
        cols = slice(f * face, (f + 1) * face)
        both = dot(xs[...], ahi[:, cols], ((1,), (0,)))
        low = dot(xs[0:k, :], alo[:, cols], ((1,), (0,)))
        return both[:k] + (both[k:] + low)

    for f in range(4):
        face_start(f, basis_face(f), nbb, bs, br)
        face_start(f, gap.at[0, 0, f], nbgap, gs, gr)
    zero_face = jnp.zeros((k, face), F32)
    for f in range(4):
        @pl.when(jnp.logical_not(has_nb[f]))
        def _():
            nbb[f] = jnp.zeros((mdev, face), F32)
            nbgap[f] = zero_face
            halo_in[f] = zero_face
            nbamps[f] = jnp.zeros((k // 2, 2 * mdev), F32)
    c_hi, c_lo = split(cinv[...])
    chi[...] = c_hi
    clo[...] = c_lo
    for f in range(4):
        hi, lo = split(basis[0, 0, f])
        bhi[f, 0:mdev] = hi
        blo[f, 0:mdev] = lo
    amps = coarse(0, crhs[0, 0])
    for f in range(4):
        face_wait(f, basis_face(f), nbb, bs, br)
        face_wait(f, gap.at[0, 0, f], nbgap, gs, gr)
        hi, lo = split(nbb[f])
        bhi[f, mdev:2 * mdev] = hi
        blo[f, mdev:2 * mdev] = lo
        dvec[f] = gap[0, 0, f] + nbgap[f]
        m = expand_sum(amps, f)
        m_out[0, 0, f] = m
        put_split(m, f)

    def a_split(i, carry):
        a_copy(i).wait()
        rows = pl.ds(pl.multiple_of(i * step_rows, step_rows), step_rows)
        hi, lo = split(stage[rows, :])
        ahi[rows, :] = hi
        alo[rows, :] = lo
        return carry

    lax.fori_loop(0, n_blocks, a_split, 0)

    lane = lax.broadcasted_iota(jnp.int32, (k, width), 1)
    sub = lax.broadcasted_iota(jnp.int32, (k, width), 0)

    own_hi = jnp.concatenate([bhi[f, 0:mdev] for f in range(4)], axis=1)
    own_lo = jnp.concatenate([blo[f, 0:mdev] for f in range(4)], axis=1)
    own = jnp.concatenate([own_hi, own_lo], axis=0)
    for g in range(4):
        cols = slice(g * face, (g + 1) * face)
        am[g] = apply_face(g)
        both = dot(own, ahi[:, cols], ((1,), (0,)))
        low = dot(own_hi, alo[:, cols], ((1,), (0,)))
        hi, lo = split(both[:mdev] + (both[mdev:] + low))
        whi[0:mdev, cols] = hi
        wlo[0:mdev, cols] = lo
        for f in range(4):
            rows = slice(f * face, (f + 1) * face)
            nb_hi, nb_lo = bhi[f, mdev:2 * mdev], blo[f, mdev:2 * mdev]
            both = dot(jnp.concatenate([nb_hi, nb_lo], axis=0), ahi[rows, cols], ((1,), (0,)))
            low = dot(nb_hi, alo[rows, cols], ((1,), (0,)))
            hi, lo = split(both[:mdev] + (both[mdev:] + low))
            whi[(f + 1) * mdev:(f + 2) * mdev, cols] = hi
            wlo[(f + 1) * mdev:(f + 2) * mdev, cols] = lo

    def group_sum(buf, ssem, rsem, at, count, where):
        copies = []
        for d in range(1, count):
            copies.append(remote(buf.at[at], buf.at[at], ssem.at[d], rsem.at[d], where(lax.rem(at + d, count))))
            copies[-1].start()
        for copy in copies:
            copy.wait()
        return jnp.sum(buf[...], axis=0)

    def iteration(step, carry):
        for f in range(4):
            face_start(f, am.at[f], halo_in, hs, hr)
        e = jnp.zeros((k, mdev), F32)
        for f in range(4):
            face_wait(f, am.at[f], halo_in, hs, hr)
            g = am[f] + halo_in[f] - dvec[f]
            grad[f] = g
            put_split(g, f)
            e = e + dot3(g, bhi[f, 0:mdev], blo[f, 0:mdev], ((1,), (1,)))

        def first():
            image[0] = apply_face(0)
            image[1] = apply_face(1)

        def second():
            image[2] = apply_face(2)

        def third():
            image[3] = apply_face(3)

        amps = coarse(1, e, first, second, third)
        every = unpack([amps] + [nbamps[f] for f in range(4)])
        numer = jnp.zeros((k, 1), F32)
        denom = jnp.zeros((k, 1), F32)
        for f in range(4):
            cols = slice(f * face, (f + 1) * face)
            g = grad[f]
            p = g - expand_sum(amps, f)
            p_out[0, 0, f] = p
            weight = jnp.where(has_nb[f], 0.5, 1.0).astype(F32)
            numer = numer + weight * jnp.sum(g * p, axis=1, keepdims=True)
            im = image[f] - dot3(every, whi[:, cols], wlo[:, cols], ((1,), (0,)))
            image[f] = im
            denom = denom + jnp.sum(p * im, axis=1, keepdims=True)
        packed = jnp.where(lane == sub, numer, 0.0) + jnp.where(lane == sub + k, denom, 0.0)
        red_a[row] = jnp.sum(packed, axis=0, keepdims=True)
        red_b[col] = group_sum(red_a, ras, rar, row, n_rows, lambda t: (t, col))
        total = group_sum(red_b, rbs, rbr, col, n_cols, lambda t: (row, t))
        numer_all = jnp.sum(jnp.where(lane == sub, total, 0.0), axis=1, keepdims=True)
        denom_all = jnp.sum(jnp.where(lane == sub + k, total, 0.0), axis=1, keepdims=True)
        ratio = numer_all / denom_all
        for f in range(4):
            am[f] = am[f] - ratio * image[f]
            linear = m_out[0, 0, f] - ratio * p_out[0, 0, f]
            contact = jnp.where(has_nb[f], 0, mask[0, 0, f:f + 1, :])
            m = jnp.where(contact == 1, jnp.maximum(linear, 0.0), linear)
            m_out[0, 0, f] = m
            put_split(m - linear, f)
        for f in range(4):
            @pl.when(jnp.logical_and(jnp.logical_not(has_nb[f]), step < ITERS - 1))
            def _():
                rows = slice(f * face, (f + 1) * face)
                change = xs[:, rows]
                for g in range(4):
                    cols = slice(g * face, (g + 1) * face)
                    both = dot(change, ahi[rows, cols], ((1,), (0,)))
                    low = dot(change[0:k], alo[rows, cols], ((1,), (0,)))
                    am[g] = am[g] + (both[:k] + (both[k:] + low))
        return carry

    lax.fori_loop(0, ITERS, iteration, 0)


def solution(mesh):
    n_rows, n_cols = mesh.shape["row"], mesh.shape["col"]

    def shards(dual_ops, basis, coarse_inverse, gap_rhs, coarse_rhs, contact_mask):
        m_len = dual_ops.shape[-1]
        _, _, _, k, face = gap_rhs.shape
        mdev = basis.shape[3]
        width = -(-2 * k // 128) * 128
        blocks = math.gcd(m_len, 32)
        vm = pltpu.VMEM
        dma = pltpu.SemaphoreType.DMA
        small = (k // 2, 2 * mdev)
        faces = vm((4, k, face), F32)
        out = jax.ShapeDtypeStruct(gap_rhs.shape, F32)
        in_vmem = pl.BlockSpec(memory_space=pltpu.VMEM)
        return pl.pallas_call(
            functools.partial(kernel, n_rows, n_cols),
            out_shape=(out, out),
            in_specs=[pl.BlockSpec(memory_space=pl.ANY)] + [in_vmem] * 5,
            out_specs=(in_vmem, in_vmem),
            scratch_shapes=[
                vm((m_len, m_len), F32), vm((m_len, m_len), BF16), vm((m_len, m_len), BF16),
                vm((4, 2 * mdev, face), BF16), vm((4, 2 * mdev, face), BF16),
                vm(coarse_inverse.shape, BF16), vm(coarse_inverse.shape, BF16),
                vm((4, mdev, face), F32), faces, faces, faces, faces, faces, faces,
                vm((2 * k, m_len), BF16), vm((5 * mdev, m_len), BF16), vm((5 * mdev, m_len), BF16),
                vm((2, n_rows, *small), F32), vm((n_cols, *small), F32), vm((2, n_cols, *small), F32),
                vm(small, F32), vm((4, *small), F32), vm((n_rows, 1, width), F32), vm((n_cols, 1, width), F32),
                dma((blocks,)),
                dma((4,)), dma((4,)), dma((4,)), dma((4,)), dma((4,)), dma((4,)),
                dma((2, n_rows)), dma((2, n_rows)), dma((2, n_cols)), dma((2, n_cols)),
                dma((4,)), dma((4,)), dma((n_rows,)), dma((n_rows,)), dma((n_cols,)), dma((n_cols,)),
            ],
            compiler_params=pltpu.CompilerParams(
                collective_id=0, has_side_effects=True, vmem_limit_bytes=60 * 1024 * 1024),
        )(dual_ops, basis, coarse_inverse, gap_rhs, coarse_rhs, contact_mask)

    return jax.shard_map(
        shards,
        mesh=mesh,
        in_specs=(
            P("row", "col", None, None),
            P("row", "col", None, None, None),
            P("row", "col"),
            P("row", "col", None, None, None),
            P("row", "col", None, None),
            P("row", "col", None, None),
        ),
        out_specs=(P("row", "col", None, None, None), P("row", "col", None, None, None)),
        check_vma=False,
    )
```

time: 944 us -> 172 us (0.18)
  blocking collectives: 454 us -> 0 us
  matrix products: 292 us -> 0 us
  Pallas kernels: 0 us -> 168 us
  starting transfers between devices: 124 us -> 0 us
  waiting for transfers between devices: 40.5 us -> 0 us
  local copies, waits for them, and re-layouts: 23.6 us -> 3.34 us
    psum x13 -> x0, blocking collectives: 373 us -> none  [the longest x6 249 us: shards(): numer_all, denom_all = lax.psum((numer, denom), ('row', 'col'))]
    dot_general x32 -> x0, matrix products: 292 us -> none  [the longest x12 281 us: apply_dual(): return jnp.einsum('gjfi,fki->gkj', blocks, vector, precision=HIGH)]
    pallas_call x0 -> x1, Pallas kernels: none -> 168 us  [shards(): pl.pallas_call(functools.partial(kernel, n_rows, n_cols), out_shape=(out,...]
    ppermute x56 -> x0, starting transfers between devices: 124 us -> none  [the longest x28 87.3 us: padded(): lax.ppermute(lax.slice_in_dim(block, block.shape[dim] - width, None, axis...]
    all_gather x7 -> x0, blocking collectives: 80.8 us -> none  [coarse(): gathered = lax.all_gather(coef, 'row', axis=1, tiled=True)]
    ppermute x56 -> x0, waiting for transfers between devices: 40.5 us -> none  [the longest x28 34 us: padded(): lax.ppermute(lax.slice_in_dim(block, 0, width, axis=dim), axis, backward)]
    another operation x1 -> x0, local copies, waits for them, and re-layouts: 20.4 us -> none  [shards(): blocks = dual_ops[0, 0].reshape(4, face_len, 4, face_len)]
  transfers between devices with their start and end apart: 56 -> 0, of which waited for: 24 -> 0; matrix products, arithmetic and copies ran while one was open for 5% -> 0% of each run, Pallas kernels for 0% -> 0%
where the time goes in v1:
time: 172 us
  Pallas kernels  168 us (98%)
  local copies, waits for them, and re-layouts  3.34 us (2%)
    pallas_call x1, Pallas kernels, shards(): pl.pallas_call(functools.partial(kernel, n_rows, n_cols), out_shape=(out,...  168 us

profile of v1, /device:TPU:0, one launch (start us, length us, event | category | flops | bytes accessed | tf_op | source)
XLA Modules:
  0.0 171.5 jit_solution(3075928201375614757)
XLA Ops:
  0.6 167.5 %shard_map.77 = (f32[1,1,4,32,512]{4,3,2,1,0:T(8,128)}, f32[1,1,4,32,512]{4,3,2,1,0:T(8,128)}) custom-call(f32[1,1,2048,2048]{3,2,1,0:T(8,128)} %a_hbm.1, f32[1,1,4,64,512]{4,3,2,1,0:T(8,128)} %basis.1, f32[256,512]{1,0:T(8,128)} %cinv.1, f32[1,1,4,32,512]{4,3,2,1,0:T(8,128)} %gap.1, f32[1,1,32,64]{3,2,1,0:T(8,128)} %crhs.1, s32[1,1,4,512]{3,2,1,0:T(4,128)} %mask.1), custom_call_target="tpu_custom_call" | custom-call | tf_op jit(solution)/shard_map/pallas_call | solution.py:296
  168.2 1.7 copy.10
  169.8 1.7 copy.11
